TPU v7x, 32 devices: a whole 2x2x4 slice. The times are simulated.
32 devices in a mesh: seq: 8 (over z, core), grp: 4 (over y, x).
Axes of the slice: x: 2, y: 2, z: 4, core: 2. Of those that a mesh axis runs over, the one named last changes fastest.
Arguments:
- tokens: bfloat16 [65536, 1280], P(('seq', 'grp')), may hold values from -27 to 27
- slot_keys: bfloat16 [1280, 128], replicated, may hold values from -1.5 to 1.5
- norm_gain: float32 [32, 1280], P(('seq', 'grp')), may hold values from 0.1 to 1.9
- w_in: bfloat16 [32, 1280, 2560], P(('seq', 'grp')), may hold values from -0.15625 to 0.15625
- w_out: bfloat16 [32, 2560, 1280], P(('seq', 'grp')), may hold values from -0.125 to 0.125
Outputs:
- mixed: bfloat16 [65536, 1280], P(('seq', 'grp'))
All inputs are finite; a program needn't handle non-finite values.
Results may differ from a plain program's by a relative error of at most 0.007.
Values may be sent and summed in bfloat16 or wider, within the bound.
No kernel may reach another device: no remote copies, remote signals or barrier semaphores. Data moves between devices by JAX's collectives and lax.ppermute only.
A program may use at most 128 MiB of HBM per device.

v0:
```python
import jax
import jax.numpy as jnp
from jax import lax
from jax.sharding import PartitionSpec as P


def on_device(tokens, slot_keys, norm_gain, w_in, w_out):
    devices = lax.axis_size(("seq", "grp"))
    logits = jnp.dot(tokens, slot_keys, preferred_element_type=jnp.float32)
    per_dev = logits.shape[1] // devices
    maxima = jnp.max(logits, axis=0)
    scores = jnp.exp(logits - maxima[None, :])
    totals = jnp.sum(scores, axis=0)
    weights = scores.astype(jnp.bfloat16)
    dims = (((0,), (0,)), ((), ()))
    numer_local = lax.dot_general(weights, tokens, dims, preferred_element_type=jnp.float32)
    parts, peaks, sums = (
        lax.all_to_all(numer_local, ("seq", "grp"), split_axis=0, concat_axis=0, tiled=True),
        lax.all_to_all(maxima, ("seq", "grp"), split_axis=0, concat_axis=0, tiled=True),
        lax.all_to_all(totals, ("seq", "grp"), split_axis=0, concat_axis=0, tiled=True),
    )
    peaks = peaks.reshape(devices, per_dev)
    factor = jnp.exp(peaks - jnp.max(peaks, axis=0, keepdims=True))
    numer = jnp.sum(parts.reshape(devices, per_dev, -1) * factor[:, :, None], axis=0)
    own_total = jnp.sum(sums.reshape(devices, per_dev) * factor, axis=0)
    slot_in = numer / own_total[:, None]
    normed = (slot_in * norm_gain[0][None, :]).astype(jnp.bfloat16)
    hidden = jax.nn.gelu(jnp.dot(normed, w_in[0], preferred_element_type=jnp.float32)).astype(
        jnp.bfloat16
    )
    expert_out = jnp.dot(hidden, w_out[0], preferred_element_type=jnp.float32).astype(jnp.bfloat16)
    row_top = jnp.max(logits, axis=1, keepdims=True)
    row_exp = jnp.exp(logits - row_top)
    combine = (row_exp / jnp.sum(row_exp, axis=1, keepdims=True)).astype(jnp.bfloat16)
    gathered = lax.all_gather(expert_out, ("seq", "grp"), axis=0, tiled=True)
    mixed = jnp.dot(combine, gathered, preferred_element_type=jnp.float32)
    return mixed.astype(jnp.bfloat16)


def solution(mesh):
    return jax.shard_map(
        on_device,
        mesh=mesh,
        in_specs=(
            P(("seq", "grp"), None),
            P(),
            P(("seq", "grp"), None),
            P(("seq", "grp"), None, None),
            P(("seq", "grp"), None, None),
        ),
        out_specs=P(("seq", "grp"), None),
        check_vma=False,
    )
```

profile of v0, /device:TPU:0, one launch (start us, length us, event | category | flops | bytes accessed | tf_op | source)
XLA Modules:
  0.0 129.9 jit_solution(6131586817786573005)
XLA Ops:
  0.0 0.0 copy-start
  0.0 1.0 copy-done
  1.0 4.1 %fusion.47 = (f32[2048]{0:T(1024)S(1)}, f32[128]{0:T(128)S(1)}, f32[2048,128]{1,0:T(8,128)S(1)}) fusion(bf16[2048,1280]{1,0:T(8,128)(2,1)} %param.5, bf16[1280,128]{1,0:T(8,128)(2,1)S(1)} %copy-done), kind=kOutput, calls=%fused_computation.43 | convolution fusion | flops 671610752 | bytes 6627840 | tf_op jit(solution)/shard_map/dot_general | solution.py:9
  5.1 0.0 copy-start.1
  5.1 0.6 fusion.10
  5.7 0.7 all_to_all.22
  6.4 7.3 %all-to-all-start.2 = ((f32[32,4,1]{1,2,0:T(1,128)}), f32[32,4,1]{1,2,0:T(1,128)S(1)}, u32[]{:S(2)}, u32[]{:S(2)}) async-start(f32[32,4,1]{1,2,0:T(1,128)} %bitcast.2), calls=%async_computation.2 | async-start | bytes 32768 | tf_op jit(solution)/shard_map/all_to_all | solution.py:20
  13.8 0.7 all_to_all.20
  14.5 6.4 %all-to-all-done.2 = f32[32,4,1]{1,2,0:T(1,128)S(1)} async-done(((f32[32,4,1]{1,2,0:T(1,128)}), f32[32,4,1]{1,2,0:T(1,128)S(1)}, u32[]{:S(2)}, u32[]{:S(2)}) %all-to-all-start.2) | async-done | bytes 544 | tf_op jit(solution)/shard_map/all_to_all | solution.py:20
  20.9 2.6 %all-to-all-start.1 = ((f32[32,4,1]{1,2,0:T(1,128)}), f32[32,4,1]{1,2,0:T(1,128)S(1)}, u32[]{:S(2)}, u32[]{:S(2)}) async-start(f32[32,4,1]{1,2,0:T(1,128)} %bitcast), calls=%async_computation.1 | async-start | bytes 32768 | tf_op jit(solution)/shard_map/all_to_all | solution.py:19
  23.4 3.4 %fusion.13 = f32[128,1280]{1,0:T(8,128)S(1)} fusion(bf16[2048,1280]{1,0:T(8,128)(2,1)} %param.5, f32[2048,128]{1,0:T(8,128)S(1)} %get-tuple-element.9, f32[128]{0:T(128)S(1)} %get-tuple-element.8), kind=kOutput, calls=%fused_computation.14 | convolution fusion | flops 671612928 | bytes 6947328 | tf_op jit(solution)/shard_map/dot_general | solution.py:16
  26.9 1.0 all_to_all.18
  27.9 2.8 %all-to-all-done.1 = f32[32,4,1]{1,2,0:T(1,128)S(1)} async-done(((f32[32,4,1]{1,2,0:T(1,128)}), f32[32,4,1]{1,2,0:T(1,128)S(1)}, u32[]{:S(2)}, u32[]{:S(2)}) %all-to-all-start.1) | async-done | bytes 544 | tf_op jit(solution)/shard_map/all_to_all | solution.py:19
  30.6 3.1 %all-to-all-start = ((f32[32,4,1280]{2,1,0:T(4,128)}), f32[32,4,1280]{2,1,0:T(4,128)S(1)}, u32[]{:S(2)}, u32[]{:S(2)}) async-start(f32[32,4,1280]{2,1,0:T(4,128)} %all_to_all.18), calls=%async_computation | async-start | bytes 1310720 | tf_op jit(solution)/shard_map/all_to_all | solution.py:18
  33.7 0.0 copy-done.1
  33.8 0.1 copy.21
  33.8 0.1 reduce_max.29
  33.9 0.1 exponential_bitcast_fusion
  34.0 0.1 copy.22
  34.1 0.1 copy.24
  34.1 0.2 fusion.42
  34.3 18.3 %all-to-all-done = f32[32,4,1280]{2,1,0:T(4,128)S(1)} async-done(((f32[32,4,1280]{2,1,0:T(4,128)}), f32[32,4,1280]{2,1,0:T(4,128)S(1)}, u32[]{:S(2)}, u32[]{:S(2)}) %all-to-all-start) | async-done | bytes 655392 | tf_op jit(solution)/shard_map/all_to_all | solution.py:18
  52.6 0.2 multiply_reduce_fusion
  52.8 6.7 %fusion.7 = bf16[1,4,1280]{2,1,0:T(4,128)(2,1)S(1)} fusion(bf16[1,2560,1280]{2,1,0:T(8,128)(2,1)} %param.9, bf16[1,1280,2560]{2,1,0:T(8,128)(2,1)} %param.8, f32[4,1280]{1,0:T(4,128)S(1)} %multiply_reduce_fusion, f32[1280]{0:T(1024)S(1)} %reduce.1, f32[4]{0:T(128)S(1)} %fusion.42), kind=kOutput, calls=%fused_computation.6 | convolution fusion | flops 52541440 | bytes 13143056 | tf_op jit(solution)/shard_map/dot_general | solution.py:31
  59.5 66.8 %all-gather = bf16[32,4,1280]{2,1,0:T(4,128)(2,1)S(1)} all-gather(bf16[1,4,1280]{2,1,0:T(4,128)(2,1)S(1)} %fusion.7), channel_id=1, replica_groups=mesh['seq'=8,'grp'=4] {'seq','grp'}, dimensions={0}, use_global_device_ids=true | all-gather | bytes 337920 | tf_op jit(solution)/shard_map/all_gather | solution.py:35
  126.3 0.1 reshape.31
  126.3 3.6 %convolution_convert_fusion = bf16[2048,1280]{1,0:T(8,128)(2,1)} fusion(bf16[128,1280]{1,0:T(8,128)(2,1)S(1)} %reshape.31, f32[2048,128]{1,0:T(8,128)S(1)} %get-tuple-element.9, f32[2048]{0:T(1024)S(1)} %get-tuple-element.5, f32[2048]{0:T(1024)S(1)} %get-tuple-element.7), kind=kOutput, calls=%fused_computation | convolution fusion | flops 674496512 | bytes 6635520 | tf_op jit(solution)/shard_map/dot_general | solution.py:36
  (1 shorter events, 0.0 us)
Async XLA Ops:
  0.0 1.0 copy-start
  5.1 28.7 %copy-start.1 = (f32[1,1280]{1,0:T(1,128)S(1)}, f32[1,1280]{1,0:T(1,128)}, u32[]{:S(2)}) copy-start(f32[1,1280]{1,0:T(1,128)} %param.7) | copy-start | bytes 15364
  6.4 14.5 %all-to-all-start.2 = ((f32[32,4,1]{1,2,0:T(1,128)}), f32[32,4,1]{1,2,0:T(1,128)S(1)}, u32[]{:S(2)}, u32[]{:S(2)}) async-start(f32[32,4,1]{1,2,0:T(1,128)} %bitcast.2), calls=%async_computation.2 | async-start | bytes 32768 | tf_op jit(solution)/shard_map/all_to_all | solution.py:20
  20.9 9.8 %all-to-all-start.1 = ((f32[32,4,1]{1,2,0:T(1,128)}), f32[32,4,1]{1,2,0:T(1,128)S(1)}, u32[]{:S(2)}, u32[]{:S(2)}) async-start(f32[32,4,1]{1,2,0:T(1,128)} %bitcast), calls=%async_computation.1 | async-start | bytes 32768 | tf_op jit(solution)/shard_map/all_to_all | solution.py:19
  30.6 21.9 %all-to-all-start = ((f32[32,4,1280]{2,1,0:T(4,128)}), f32[32,4,1280]{2,1,0:T(4,128)S(1)}, u32[]{:S(2)}, u32[]{:S(2)}) async-start(f32[32,4,1280]{2,1,0:T(4,128)} %all_to_all.18), calls=%async_computation | async-start | bytes 1310720 | tf_op jit(solution)/shard_map/all_to_all | solution.py:18
where the time goes:
time: 130 us
  blocking collectives  66.8 us (51%)
  waiting for transfers between devices  27.4 us (21%)
  matrix products  17.8 us (14%)
  starting transfers between devices  13 us (10%)
  local copies, waits for them, and re-layouts  3.74 us (3%)
    all_gather x1, blocking collectives, on_device(): gathered = lax.all_gather(expert_out, ('seq', 'grp'), axis=0, tiled=True)  66.8 us
    all_to_all x1, waiting for transfers between devices, on_device(): lax.all_to_all(numer_local, ('seq', 'grp'), split_axis=0, concat_axis=0,...  18.3 us
    all_to_all x1, starting transfers between devices, on_device(): lax.all_to_all(totals, ('seq', 'grp'), split_axis=0, concat_axis=0, tiled...  7.32 us
    dot_general x1, matrix products, on_device(): jnp.dot(hidden, w_out[0], preferred_element_type=jnp.float32)  6.7 us
    all_to_all x1, waiting for transfers between devices, on_device(): lax.all_to_all(totals, ('seq', 'grp'), split_axis=0, concat_axis=0, tiled...  6.42 us
    dot_general x1, matrix products, on_device(): logits = jnp.dot(tokens, slot_keys, preferred_element_type=jnp.float32)  4.08 us
    dot_general x1, matrix products, on_device(): mixed = jnp.dot(combine, gathered, preferred_element_type=jnp.float32)  3.58 us
    dot_general x1, matrix products, on_device(): lax.dot_general(weights, tokens, dims, preferred_element_type=jnp.float32)  3.4 us
  transfers between devices with their start and end apart: 3, of which 3 were waited for; matrix products, arithmetic and copies ran while one was open for 3% of the time, Pallas kernels for 0%

commit v1 on v0

--- a/solution.py
+++ b/solution.py
@@ -32,7 +32,17 @@
     row_top = jnp.max(logits, axis=1, keepdims=True)
     row_exp = jnp.exp(logits - row_top)
     combine = (row_exp / jnp.sum(row_exp, axis=1, keepdims=True)).astype(jnp.bfloat16)
-    gathered = lax.all_gather(expert_out, ("seq", "grp"), axis=0, tiled=True)
+    value_now, right_arr = (jax.lax.psum(1, ("seq", "grp")), jax.lax.axis_index(("seq", "grp")))
+    gathered, r_now = (expert_out, 1)
+    while r_now < value_now:
+        frames = []
+        for kk in [*range(value_now)]:
+            frames.append((kk, kk ^ r_now))
+        y_new = jax.lax.ppermute(gathered, ("seq", "grp"), perm=frames)
+        y = jnp.concatenate([gathered, y_new], axis=0)
+        local_now = jnp.concatenate([y_new, gathered], axis=0)
+        gathered = jnp.where(right_arr & r_now == 0, y, local_now)
+        r_now = 2 * r_now
     mixed = jnp.dot(combine, gathered, preferred_element_type=jnp.float32)
     return mixed.astype(jnp.bfloat16)
 

time: 130 us -> 86.8 us (0.67)
  blocking collectives: 66.8 us -> 0 us
  waiting for transfers between devices: 27.4 us -> 48.3 us
  starting transfers between devices: 13 us -> 15.4 us
    all_gather x1 -> x0, blocking collectives: 66.8 us -> none  [on_device(): gathered = lax.all_gather(expert_out, ('seq', 'grp'), axis=0, tiled=True)]
    ppermute x0 -> x5, waiting for transfers between devices: none -> 20.9 us  [on_device(): y_new = jax.lax.ppermute(gathered, ('seq', 'grp'), perm=frames)]
    ppermute x0 -> x5, starting transfers between devices: none -> 2.41 us  [on_device(): y_new = jax.lax.ppermute(gathered, ('seq', 'grp'), perm=frames)]
  transfers between devices with their start and end apart: 3 -> 8, of which waited for: 3 -> 8; matrix products, arithmetic and copies ran while one was open for 3% -> 5% of each run, Pallas kernels for 0% -> 0%
where the time goes in v1:
time: 86.8 us; the launch traced here: 86.4 us
  waiting for transfers between devices  48.3 us (56%)
  matrix products  17.7 us (20%)
  starting transfers between devices  15.4 us (18%)
  local copies, waits for them, and re-layouts  3.66 us (4%)
  other arithmetic  1.25 us (1%)
    ppermute x5, waiting for transfers between devices, on_device(): y_new = jax.lax.ppermute(gathered, ('seq', 'grp'), perm=frames)  20.9 us
    all_to_all x1, waiting for transfers between devices, on_device(): lax.all_to_all(numer_local, ('seq', 'grp'), split_axis=0, concat_axis=0,...  18.3 us
    all_to_all x1, starting transfers between devices, on_device(): lax.all_to_all(totals, ('seq', 'grp'), split_axis=0, concat_axis=0, tiled...  7.32 us
    dot_general x1, matrix products, on_device(): jnp.dot(hidden, w_out[0], preferred_element_type=jnp.float32)  6.7 us
    all_to_all x1, waiting for transfers between devices, on_device(): lax.all_to_all(totals, ('seq', 'grp'), split_axis=0, concat_axis=0, tiled...  6.42 us
    dot_general x1, matrix products, on_device(): logits = jnp.dot(tokens, slot_keys, preferred_element_type=jnp.float32)  4.08 us
    dot_general x1, matrix products, on_device(): mixed = jnp.dot(combine, gathered, preferred_element_type=jnp.float32)  3.56 us
    dot_general x1, matrix products, on_device(): lax.dot_general(weights, tokens, dims, preferred_element_type=jnp.float32)  3.4 us
  transfers between devices with their start and end apart: 8, of which 8 were waited for; matrix products, arithmetic and copies ran while one was open for 5% of the time, Pallas kernels for 0%

profile of v1, /device:TPU:0, one launch (start us, length us, event | category | flops | bytes accessed | tf_op | source)
XLA Modules:
  0.0 86.4 jit_solution(7779200261501206317)
XLA Ops:
  0.0 1.0 %copy-done = bf16[1280,128]{1,0:T(8,128)(2,1)S(1)} copy-done((bf16[1280,128]{1,0:T(8,128)(2,1)S(1)}, bf16[1280,128]{1,0:T(8,128)(2,1)}, u32[]{:S(2)}) %copy-start) | copy-done | bytes 327704
  1.0 4.1 %fusion.51 = (f32[128]{0:T(128)S(1)}, f32[2048]{0:T(1024)S(1)}, f32[2048,128]{1,0:T(8,128)S(1)}) fusion(bf16[2048,1280]{1,0:T(8,128)(2,1)} %param.5, bf16[1280,128]{1,0:T(8,128)(2,1)S(1)} %copy-done), kind=kOutput, calls=%fused_computation.54 | convolution fusion | flops 671610752 | bytes 6627840 | tf_op jit(solution)/shard_map/dot_general | solution.py:9
  5.1 0.6 fusion.8
  5.7 0.7 all_to_all.22
  6.4 7.3 %all-to-all-start.2 = ((f32[32,4,1]{1,2,0:T(1,128)}), f32[32,4,1]{1,2,0:T(1,128)S(1)}, u32[]{:S(2)}, u32[]{:S(2)}) async-start(f32[32,4,1]{1,2,0:T(1,128)} %bitcast.2), calls=%async_computation.2 | async-start | bytes 32768 | tf_op jit(solution)/shard_map/all_to_all | solution.py:20
  13.8 0.7 all_to_all.20
  14.5 6.4 %all-to-all-done.2 = f32[32,4,1]{1,2,0:T(1,128)S(1)} async-done(((f32[32,4,1]{1,2,0:T(1,128)}), f32[32,4,1]{1,2,0:T(1,128)S(1)}, u32[]{:S(2)}, u32[]{:S(2)}) %all-to-all-start.2) | async-done | bytes 544 | tf_op jit(solution)/shard_map/all_to_all | solution.py:20
  20.9 2.6 %all-to-all-start.1 = ((f32[32,4,1]{1,2,0:T(1,128)}), f32[32,4,1]{1,2,0:T(1,128)S(1)}, u32[]{:S(2)}, u32[]{:S(2)}) async-start(f32[32,4,1]{1,2,0:T(1,128)} %bitcast), calls=%async_computation.1 | async-start | bytes 32768 | tf_op jit(solution)/shard_map/all_to_all | solution.py:19
  23.4 3.4 %fusion.10 = f32[128,1280]{1,0:T(8,128)S(1)} fusion(bf16[2048,1280]{1,0:T(8,128)(2,1)} %param.5, f32[2048,128]{1,0:T(8,128)S(1)} %get-tuple-element.9, f32[128]{0:T(128)S(1)} %get-tuple-element.7), kind=kOutput, calls=%fused_computation.13 | convolution fusion | flops 671612928 | bytes 6947328 | tf_op jit(solution)/shard_map/dot_general | solution.py:16
  26.9 1.0 %all_to_all.18 = f32[32,4,1280]{2,1,0:T(4,128)} reshape(f32[128,1280]{1,0:T(8,128)S(1)} %fusion.10) | data formatting | bytes 1310720 | tf_op jit(solution)/shard_map/all_to_all | solution.py:18
  27.9 2.8 %all-to-all-done.1 = f32[32,4,1]{1,2,0:T(1,128)S(1)} async-done(((f32[32,4,1]{1,2,0:T(1,128)}), f32[32,4,1]{1,2,0:T(1,128)S(1)}, u32[]{:S(2)}, u32[]{:S(2)}) %all-to-all-start.1) | async-done | bytes 544 | tf_op jit(solution)/shard_map/all_to_all | solution.py:19
  30.6 3.1 %all-to-all-start = ((f32[32,4,1280]{2,1,0:T(4,128)}), f32[32,4,1280]{2,1,0:T(4,128)S(1)}, u32[]{:S(2)}, u32[]{:S(2)}) async-start(f32[32,4,1280]{2,1,0:T(4,128)} %all_to_all.18), calls=%async_computation | async-start | bytes 1310720 | tf_op jit(solution)/shard_map/all_to_all | solution.py:18
  33.8 0.1 copy.21
  33.8 0.1 reduce_max.29
  33.9 0.1 exponential_bitcast_fusion
  34.0 0.1 copy.22
  34.1 0.1 copy.24
  34.1 0.2 fusion.45
  34.3 18.3 %all-to-all-done = f32[32,4,1280]{2,1,0:T(4,128)S(1)} async-done(((f32[32,4,1280]{2,1,0:T(4,128)}), f32[32,4,1280]{2,1,0:T(4,128)S(1)}, u32[]{:S(2)}, u32[]{:S(2)}) %all-to-all-start) | async-done | bytes 655392 | tf_op jit(solution)/shard_map/all_to_all | solution.py:18
  52.6 0.2 multiply_reduce_fusion
  52.8 6.7 %fusion.4 = bf16[4,1280]{1,0:T(4,128)(2,1)S(1)} fusion(bf16[1,2560,1280]{2,1,0:T(8,128)(2,1)} %param.9, bf16[1,1280,2560]{2,1,0:T(8,128)(2,1)} %param.8, f32[4,1280]{1,0:T(4,128)S(1)} %multiply_reduce_fusion, f32[1280]{0:T(1024)S(1)} %reduce.1, f32[4]{0:T(128)S(1)} %fusion.45), kind=kOutput, calls=%fused_computation.5 | convolution fusion | flops 52541440 | bytes 13143056 | tf_op jit(solution)/shard_map/dot_general | solution.py:31
  59.5 0.4 collective-permute-start
  59.9 3.3 %collective-permute-done = bf16[4,1280]{1,0:T(4,128)(2,1)S(1)} collective-permute-done((bf16[4,1280]{1,0:T(4,128)(2,1)S(1)}, bf16[4,1280]{1,0:T(4,128)(2,1)S(1)}, u32[]{:S(2)}, u32[]{:S(2)}) %collective-permute-start) | collective-permute-done | bytes 10272 | tf_op jit(solution)/shard_map/ppermute | solution.py:41
  63.2 0.5 collective-permute-start.1
  63.7 3.4 %collective-permute-done.1 = bf16[8,1280]{1,0:T(8,128)(2,1)S(1)} collective-permute-done((bf16[8,1280]{1,0:T(8,128)(2,1)S(1)}, bf16[8,1280]{1,0:T(8,128)(2,1)S(1)}, u32[]{:S(2)}, u32[]{:S(2)}) %collective-permute-start.1) | collective-permute-done | bytes 20512 | tf_op jit(solution)/shard_map/ppermute | solution.py:41
  67.1 0.1 collective-permute-start.2
  67.2 1.2 %collective-permute-done.2 = bf16[16,1280]{1,0:T(8,128)(2,1)S(1)} collective-permute-done((bf16[16,1280]{1,0:T(8,128)(2,1)S(1)}, bf16[16,1280]{1,0:T(8,128)(2,1)S(1)}, u32[]{:S(2)}, u32[]{:S(2)}) %collective-permute-start.2) | collective-permute-done | bytes 40992 | tf_op jit(solution)/shard_map/ppermute | solution.py:41
  68.4 1.2 %collective-permute-start.3 = (bf16[32,1280]{1,0:T(8,128)(2,1)S(1)}, bf16[32,1280]{1,0:T(8,128)(2,1)S(1)}, u32[]{:S(2)}, u32[]{:S(2)}) collective-permute-start(bf16[32,1280]{1,0:T(8,128)(2,1)S(1)} %maximum_select_fusion.3), channel_id=1, source_target_pairs={{0,8},{1,9},{2,10},{3,11},{4,12},{5,13},{6,14},{7,15},{8,0},{9,1},... | collective-permute-start | bytes 245768 | tf_op jit(solution)/shard_map/ppermute | solution.py:41
  69.5 3.4 %collective-permute-done.3 = bf16[32,1280]{1,0:T(8,128)(2,1)S(1)} collective-permute-done((bf16[32,1280]{1,0:T(8,128)(2,1)S(1)}, bf16[32,1280]{1,0:T(8,128)(2,1)S(1)}, u32[]{:S(2)}, u32[]{:S(2)}) %collective-permute-start.3) | collective-permute-done | bytes 81952 | tf_op jit(solution)/shard_map/ppermute | solution.py:41
  73.0 0.3 collective-permute-start.4
  73.3 9.6 %collective-permute-done.4 = bf16[64,1280]{1,0:T(8,128)(2,1)S(1)} collective-permute-done((bf16[64,1280]{1,0:T(8,128)(2,1)S(1)}, bf16[64,1280]{1,0:T(8,128)(2,1)S(1)}, u32[]{:S(2)}, u32[]{:S(2)}) %collective-permute-start.4) | collective-permute-done | bytes 163872 | tf_op jit(solution)/shard_map/ppermute | solution.py:41
  82.9 3.6 %convolution_convert_fusion = bf16[2048,1280]{1,0:T(8,128)(2,1)} fusion(f32[2048,128]{1,0:T(8,128)S(1)} %get-tuple-element.9, f32[2048]{0:T(1024)S(1)} %get-tuple-element.6, f32[2048]{0:T(1024)S(1)} %get-tuple-element.8, bf16[64,1280]{1,0:T(8,128)(2,1)S(1)} %collective-permute-done.4, bf16[64,1280]{1,0:T(8,128)(2,1)S(1)} %maximum_select_fusion.2, pred[]{:T(512)S(6)} %eq.15), kind=kOutput, calls=%fused_computation | convolution fusion | flops 675971072 | bytes 6635521 | tf_op jit(solution)/shard_map/dot_general | solution.py:46
  (8 shorter events, 0.1 us)
Async XLA Ops:
  0.0 1.0 %copy-start = (bf16[1280,128]{1,0:T(8,128)(2,1)S(1)}, bf16[1280,128]{1,0:T(8,128)(2,1)}, u32[]{:S(2)}) copy-start(bf16[1280,128]{1,0:T(8,128)(2,1)} %param.6) | copy-start | bytes 983044
  5.1 28.7 %copy-start.1 = (f32[1,1280]{1,0:T(1,128)S(1)}, f32[1,1280]{1,0:T(1,128)}, u32[]{:S(2)}) copy-start(f32[1,1280]{1,0:T(1,128)} %param.7) | copy-start | bytes 15364
  6.4 14.5 %all-to-all-start.2 = ((f32[32,4,1]{1,2,0:T(1,128)}), f32[32,4,1]{1,2,0:T(1,128)S(1)}, u32[]{:S(2)}, u32[]{:S(2)}) async-start(f32[32,4,1]{1,2,0:T(1,128)} %bitcast.2), calls=%async_computation.2 | async-start | bytes 32768 | tf_op jit(solution)/shard_map/all_to_all | solution.py:20
  20.9 9.8 %all-to-all-start.1 = ((f32[32,4,1]{1,2,0:T(1,128)}), f32[32,4,1]{1,2,0:T(1,128)S(1)}, u32[]{:S(2)}, u32[]{:S(2)}) async-start(f32[32,4,1]{1,2,0:T(1,128)} %bitcast), calls=%async_computation.1 | async-start | bytes 32768 | tf_op jit(solution)/shard_map/all_to_all | solution.py:19
  30.6 21.9 %all-to-all-start = ((f32[32,4,1280]{2,1,0:T(4,128)}), f32[32,4,1280]{2,1,0:T(4,128)S(1)}, u32[]{:S(2)}, u32[]{:S(2)}) async-start(f32[32,4,1280]{2,1,0:T(4,128)} %all_to_all.18), calls=%async_computation | async-start | bytes 1310720 | tf_op jit(solution)/shard_map/all_to_all | solution.py:18
  59.5 3.7 %collective-permute-start = (bf16[4,1280]{1,0:T(4,128)(2,1)S(1)}, bf16[4,1280]{1,0:T(4,128)(2,1)S(1)}, u32[]{:S(2)}, u32[]{:S(2)}) collective-permute-start(bf16[4,1280]{1,0:T(4,128)(2,1)S(1)} %fusion.4), channel_id=1, source_target_pairs={{0,1},{1,0},{2,3},{3,2},{4,5},{5,4},{6,7},{7,6},{8,9},{9,8},{10,11... | collective-permute-start | bytes 30728 | tf_op jit(solution)/shard_map/ppermute | solution.py:41
  63.2 3.8 %collective-permute-start.1 = (bf16[8,1280]{1,0:T(8,128)(2,1)S(1)}, bf16[8,1280]{1,0:T(8,128)(2,1)S(1)}, u32[]{:S(2)}, u32[]{:S(2)}) collective-permute-start(bf16[8,1280]{1,0:T(8,128)(2,1)S(1)} %maximum_select_fusion.5), channel_id=1, source_target_pairs={{0,2},{1,3},{2,0},{3,1},{4,6},{5,7},{6,4},{7,5},{8,10},{9,11},{10,... | collective-permute-start | bytes 61448 | tf_op jit(solution)/shard_map/ppermute | solution.py:41
  67.1 1.3 %collective-permute-start.2 = (bf16[16,1280]{1,0:T(8,128)(2,1)S(1)}, bf16[16,1280]{1,0:T(8,128)(2,1)S(1)}, u32[]{:S(2)}, u32[]{:S(2)}) collective-permute-start(bf16[16,1280]{1,0:T(8,128)(2,1)S(1)} %maximum_select_fusion.4), channel_id=1, source_target_pairs={{0,4},{1,5},{2,6},{3,7},{4,0},{5,1},{6,2},{7,3},{8,12},{9,13},{10,... | collective-permute-start | bytes 122888 | tf_op jit(solution)/shard_map/ppermute | solution.py:41
  68.4 4.6 %collective-permute-start.3 = (bf16[32,1280]{1,0:T(8,128)(2,1)S(1)}, bf16[32,1280]{1,0:T(8,128)(2,1)S(1)}, u32[]{:S(2)}, u32[]{:S(2)}) collective-permute-start(bf16[32,1280]{1,0:T(8,128)(2,1)S(1)} %maximum_select_fusion.3), channel_id=1, source_target_pairs={{0,8},{1,9},{2,10},{3,11},{4,12},{5,13},{6,14},{7,15},{8,0},{9,1},... | collective-permute-start | bytes 245768 | tf_op jit(solution)/shard_map/ppermute | solution.py:41
  73.0 9.9 %collective-permute-start.4 = (bf16[64,1280]{1,0:T(8,128)(2,1)S(1)}, bf16[64,1280]{1,0:T(8,128)(2,1)S(1)}, u32[]{:S(2)}, u32[]{:S(2)}) collective-permute-start(bf16[64,1280]{1,0:T(8,128)(2,1)S(1)} %maximum_select_fusion.2), channel_id=1, source_target_pairs={{0,16},{1,17},{2,18},{3,19},{4,20},{5,21},{6,22},{7,23},{8,24},{9,... | collective-permute-start | bytes 491528 | tf_op jit(solution)/shard_map/ppermute | solution.py:41
